TPU v7x, 512 devices: a whole 4x4x16 slice. The times are simulated.
512 devices in a mesh: kgrp: 16 (over y, x), energy: 32 (over z, core).
Axes of the slice: x: 4, y: 4, z: 16, core: 2. Of those that a mesh axis runs over, the one named last changes fastest.
Arguments:
- greens: float32 [2, 2, 2, 1024, 4096], P(None, None, None, 'kgrp', 'energy'), may hold values from -6 to 6
- current: float32 [2, 2, 2, 1024, 4096], P(None, None, None, ('kgrp', 'energy')), may hold values from -6 to 6
- past_inputs: float32 [5, 2, 2, 2, 1024, 4096], P(None, None, None, None, ('kgrp', 'energy')), may hold values from -6 to 6
- past_residuals: float32 [5, 2, 2, 2, 1024, 4096], P(None, None, None, None, ('kgrp', 'energy')), may hold values from -40 to 40
- slot_order: int32 [5], replicated, may hold values from 0 to 4, each once
- neighbour: int32 [1024, 5], P('kgrp'), may hold values from 0 to 1023, as said below
- momentum_class: int32 [1024], P('kgrp'), may hold values from 0 to 3
- stencil_weight: float32 [5], replicated, may hold values from 0.1 to 0.4
- acoustic_coupling: float32 [4], replicated, may hold values from 0.3 to 1.5
- optical_coupling: float32 [2], replicated, may hold values from 0.2 to 0.6
- occupation: float32 [2], replicated, may hold values from 0.1 to 1
- phonon_shift: int32 [2], replicated, may hold values from 32 to 96, as said below
Outputs:
- mixed: float32 [2, 2, 2, 1024, 4096], P(None, None, None, ('kgrp', 'energy'))
Inputs may be any that keep to these rules, and one draw needn't show every extreme that they name: `neighbour`: each index names a momentum of the row's own group of 64 consecutive momenta or of the group just before or after it, counted periodically over all groups. `phonon_shift`: the larger of the two shifts is exactly 96.
All inputs are finite; a program needn't handle non-finite values.
Results may differ from a plain program's by a relative error of at most 0.000053.
Values sent between devices are 32-bit elements; how exact they have to be, the bound alone decides.
A program may use at most 64 MiB of HBM per device.

v0:
```python
import jax
import jax.numpy as jnp
from jax import lax
from jax.sharding import PartitionSpec as P

SHIFT_MAX = 96
HIST = 5
mixing_share = 0.5
ridge_share = 0.1


def padded_2(block, sides, width, periodic):
    for axis, dim in sides:
        count = lax.axis_size(axis)
        forward = [(i, i + 1) for i in range(count - 1)]
        if periodic:
            forward.append((count - 1, 0))
        backward = [(target, source) for source, target in forward]
        low = lax.ppermute(
            lax.slice_in_dim(block, block.shape[dim] - width, None, axis=dim), axis, forward
        )
        high = lax.ppermute(lax.slice_in_dim(block, 0, width, axis=dim), axis, backward)
        block = jnp.concatenate([low, block, high], axis=dim)
    return block


def emit(padded, margin, length, coupling_row, optical, occupation, shifts):
    lesser = padded[0]
    greater = padded[1]

    def energy_view(source, offset):
        return lax.dynamic_slice_in_dim(source, margin + offset, length, axis=source.ndim - 1)

    sigma_less = coupling_row[:, None] * energy_view(lesser, 0)
    sigma_more = coupling_row[:, None] * energy_view(greater, 0)
    for column in range(2):
        strength = optical[column]
        number = occupation[column]
        offset = shifts[column]
        sigma_less = sigma_less + strength * (
            (number + 1.0) * energy_view(lesser, offset) + number * energy_view(lesser, -offset)
        )
        sigma_more = sigma_more + strength * (
            (number + 1.0) * energy_view(greater, -offset) + number * energy_view(greater, offset)
        )
    return jnp.stack([sigma_less, sigma_more])


def solve_spd(matrix, vector):
    factor = jnp.linalg.cholesky(matrix)
    size_n = matrix.shape[0]
    forward = []
    for column in range(size_n):
        summed = vector[column]
        for earlier in range(column):
            summed = summed - factor[column, earlier] * forward[earlier]
        forward.append(summed / factor[column, column])
    backward = [None] * size_n
    for column in range(size_n - 1, -1, -1):
        summed = forward[column]
        for earlier in range(column + 1, size_n):
            summed = summed - factor[earlier, column] * backward[earlier]
        backward[column] = summed / factor[column, column]
    return jnp.stack(backward)


def mix_weights(products):
    size_n = products.shape[0] - 1
    differ_rows = jnp.eye(size_n, size_n + 1, dtype=jnp.float32) - jnp.eye(
        size_n, size_n + 1, k=1, dtype=jnp.float32
    )
    system = jnp.dot(
        jnp.dot(differ_rows, products, precision=lax.Precision.HIGHEST),
        differ_rows.T,
        precision=lax.Precision.HIGHEST,
    )
    target = jnp.dot(differ_rows, products[:, 0], precision=lax.Precision.HIGHEST)
    ridge = ridge_share * jnp.trace(system) / size_n + 1e-06
    gamma = solve_spd(system + ridge * jnp.eye(size_n, dtype=jnp.float32), target)
    unit = jnp.zeros((size_n + 1,), jnp.float32).at[0].set(1.0)
    return unit - jnp.dot(differ_rows.T, gamma, precision=lax.Precision.HIGHEST)


def per_device(
    greens,
    current,
    past_inputs,
    past_residuals,
    slot_order,
    neighbour,
    momentum_class,
    stencil_weight,
    acoustic_coupling,
    optical_coupling,
    occupation,
    phonon_shift,
):
    group_len = greens.shape[3]
    slice_len = greens.shape[4]
    group_id = lax.axis_index("kgrp")
    total_k = group_len * lax.axis_size("kgrp")
    history = past_residuals.reshape(HIST, -1)
    extended = padded_2(greens, (("kgrp", 3),), group_len, True)
    local_index = (neighbour - group_id * group_len + group_len) % total_k
    smeared = jnp.zeros_like(greens)
    for column in range(5):
        smeared = smeared + stencil_weight[column] * jnp.take(
            extended, local_index[:, column], axis=3
        )
    classes = acoustic_coupling.shape[0]
    coupling_row = jnp.sum(
        jnp.where(
            momentum_class[:, None] == jnp.arange(classes, dtype=jnp.int32)[None, :],
            acoustic_coupling[None, :],
            0.0,
        ),
        axis=1,
    )
    padded = padded_2(smeared, (("energy", 4),), SHIFT_MAX, False)
    sigma_slice = emit(
        padded, SHIFT_MAX, slice_len, coupling_row, optical_coupling, occupation, phonon_shift
    )
    sigma_new = lax.all_to_all(sigma_slice, "energy", split_axis=3, concat_axis=4, tiled=True)
    residual_now = sigma_new - current
    fresh = residual_now.reshape(-1)
    new_local = jnp.concatenate(
        [jnp.sum(fresh * fresh)[None], jnp.dot(history, fresh, precision=lax.Precision.HIGHEST)]
    )
    old_products, new_products = lax.psum(
        (jnp.dot(history, history.T, precision=lax.Precision.HIGHEST), new_local),
        ("kgrp", "energy"),
    )
    entries = float(fresh.shape[0] * lax.axis_size("kgrp") * lax.axis_size("energy"))
    reorder = (slot_order[:, None] == jnp.arange(HIST, dtype=jnp.int32)[None, :]).astype(
        jnp.float32
    )
    old_aged = jnp.dot(
        jnp.dot(reorder, old_products, precision=lax.Precision.HIGHEST),
        reorder.T,
        precision=lax.Precision.HIGHEST,
    )
    new_aged = jnp.dot(reorder, new_products[1:], precision=lax.Precision.HIGHEST)
    top_row = jnp.concatenate([new_products[:1], new_aged])[None, :]
    lower_rows = jnp.concatenate([new_aged[:, None], old_aged], axis=1)
    products = jnp.concatenate([top_row, lower_rows], axis=0) / entries
    weights = mix_weights(products)
    slot_weights = jnp.dot(reorder.T, weights[1:], precision=lax.Precision.HIGHEST)
    mixed = weights[0] * (current + mixing_share * residual_now)
    for column in range(HIST):
        mixed = mixed + slot_weights[column] * (
            past_inputs[column] + mixing_share * past_residuals[column]
        )
    return mixed


def solution(mesh):
    return jax.shard_map(
        per_device,
        mesh=mesh,
        in_specs=(
            P(None, None, None, "kgrp", "energy"),
            P(None, None, None, ("kgrp", "energy"), None),
            P(None, None, None, None, ("kgrp", "energy"), None),
            P(None, None, None, None, ("kgrp", "energy"), None),
            P(),
            P("kgrp", None),
            P("kgrp"),
            P(),
            P(),
            P(),
            P(),
            P(),
        ),
        out_specs=P(None, None, None, ("kgrp", "energy"), None),
        check_vma=False,
    )
```

profile of v0, /device:TPU:1, one launch (start us, length us, event | category | flops | bytes accessed | tf_op | source)
XLA Modules:
  0.0 223.4 jit_solution(8509440534947344868)
XLA Ops:
  0.0 1.2 copy.61
  1.2 3.9 %collective-permute-start = (f32[2,2,2,64,128]{4,2,3,1,0:T(2,128)S(1)}, f32[2,2,2,64,128]{4,2,3,1,0:T(2,128)S(1)}, u32[]{:S(2)}, u32[]{:S(2)}) collective-permute-start(f32[2,2,2,64,128]{4,2,3,1,0:T(2,128)S(1)} %copy.61), channel_id=1, source_target_pairs={{0,32},{32,64},{64,96},{96,128},{128,160},{160,192},{192,224},{224... | collective-permute-start | bytes 786440 | tf_op jit(solution)/shard_map/ppermute | solution.py:19
  5.2 5.6 %collective-permute-start.1 = (f32[2,2,2,64,128]{4,2,3,1,0:T(2,128)S(1)}, f32[2,2,2,64,128]{4,2,3,1,0:T(2,128)S(1)}, u32[]{:S(2)}, u32[]{:S(2)}) collective-permute-start(f32[2,2,2,64,128]{4,2,3,1,0:T(2,128)S(1)} %copy.61), channel_id=1, source_target_pairs={{32,0},{64,32},{96,64},{128,96},{160,128},{192,160},{224,192},{256... | collective-permute-start | bytes 786440 | tf_op jit(solution)/shard_map/ppermute | solution.py:22
  10.8 0.7 add_select_fusion
  11.6 1.4 fusion.50
  12.9 1.3 fusion.49
  19.3 1.5 fusion.51
  20.8 0.0 collective-permute-done
  20.9 0.0 copy-done.2
  20.9 0.2 constant_dynamic-update-slice_fusion.1
  21.1 0.0 collective-permute-done.1
  21.2 0.9 gather_fusion.1
  22.1 0.9 gather_fusion.2
  23.0 0.9 gather_fusion.3
  23.9 0.9 gather_fusion.4
  24.8 0.9 gather_fusion
  25.7 0.0 copy-start.4
  25.8 0.0 copy-start.5
  25.8 0.0 copy-start.6
  25.8 3.5 %fusion.11 = f32[2,2,2,64,128]{4,3,2,1,0:T(8,128)S(1)} fusion(f32[64,2,2,2,128]{4,3,2,1,0:T(2,128)S(1)} %gather_fusion.4, f32[64,2,2,2,128]{4,3,2,1,0:T(2,128)S(1)} %gather_fusion.3, f32[64,2,2,2,128]{4,3,2,1,0:T(2,128)S(1)} %gather_fusion.2, f32[64,2,2,2,128]{4,3,2,1,0:T(2,128)S(1)} %gather_fusion.1, f32[64,2,2,2,128]{4,3,2,1,0:T(2,128)S(1)} %gather_fusion, ...), kind=kLoop, calls=%fused_computation.23 | loop fusion | flops 917504 | bytes 1573204 | tf_op jit(solution)/shard_map/add | solution.py:107
  29.3 0.1 fusion.44
  29.5 4.5 %collective-permute-start.2 = (f32[2,2,2,64,96]{4,3,2,1,0:T(8,128)S(1)}, f32[2,2,2,64,96]{4,3,2,1,0:T(8,128)S(1)}, u32[]{:S(2)}, u32[]{:S(2)}) collective-permute-start(f32[2,2,2,64,96]{4,3,2,1,0:T(8,128)S(1)} %get-tuple-element.36), channel_id=1, source_target_pairs={{0,1},{1,2},{2,3},{3,4},{4,5},{5,6},{6,7},{7,8},{8,9},{9,10},{10,1... | collective-permute-start | bytes 589832 | tf_op jit(solution)/shard_map/ppermute | solution.py:19
  34.0 5.2 %collective-permute-start.3 = (f32[2,2,2,64,96]{4,3,2,1,0:T(8,128)S(1)}, f32[2,2,2,64,96]{4,3,2,1,0:T(8,128)S(1)}, u32[]{:S(2)}, u32[]{:S(2)}) collective-permute-start(f32[2,2,2,64,96]{4,3,2,1,0:T(8,128)S(1)} %get-tuple-element.37), channel_id=1, source_target_pairs={{1,0},{2,1},{3,2},{4,3},{5,4},{6,5},{7,6},{8,7},{9,8},{10,9},{11,1... | collective-permute-start | bytes 589832 | tf_op jit(solution)/shard_map/ppermute | solution.py:22
  39.2 0.6 fusion.48
  39.8 0.0 copy-done.5
  39.8 0.1 select_reduce_fusion.2
  39.9 0.0 collective-permute-done.2
  39.9 1.8 collective-permute-done.3
  41.7 0.3 pad_maximum_fusion
  42.0 0.2 fusion.43
  42.2 0.0 copy-start
  42.2 3.0 %fusion.21 = (f32[1,2,2,64,128]{4,3,2,1,0:T(8,128)S(1)}, f32[1,2,2,64,128]{4,3,2,1,0:T(8,128)S(1)}) fusion(f32[2,2,64,320]{3,2,1,0:T(8,128)S(1)} %get-tuple-element.31, f32[1,2,2,64,320]{4,3,2,1,0:T(8,128)S(1)} %get-tuple-element.30, s32[]{:T(128)S(6)} %select_n.48, s32[]{:T(128)S(6)} %select_n.47, s32[]{:T(128)S(6)} %select_n.46, s32[]{:T(128)S(6)} %select_n.45, ...), kind=kLoop, calls=%fused_computation.45 | loop fusion | flops 720896 | bytes 1573160 | tf_op jit(solution)/shard_map/stack | solution.py:46
  45.2 0.9 copy.69
  46.1 15.2 %all-to-all-start = ((f32[2,2,2,64,128]{4,2,1,0,3:T(2,128)}), f32[2,2,2,64,128]{4,2,1,0,3:T(2,128)S(1)}, u32[]{:S(2)}, u32[]{:S(2)}) async-start(f32[2,2,2,64,128]{4,2,1,0,3:T(2,128)} %copy.69), calls=%async_computation | async-start | bytes 524288 | tf_op jit(solution)/shard_map/all_to_all | solution.py:123
  61.4 0.0 copy-start.3
  61.4 5.2 %fusion.4 = f32[5,5]{1,0:T(8,128)S(1)} fusion(f32[5,2,2,2,2,4096]{5,4,3,2,1,0:T(2,128)S(1)} %copy-done), kind=kOutput, calls=%fused_computation.9 | convolution fusion | flops 19660800 | bytes 1310820 | tf_op jit(solution)/shard_map/dot_general | solution.py:130
  66.5 16.8 %all-to-all-done = f32[2,2,2,64,128]{4,2,1,0,3:T(2,128)S(1)} async-done(((f32[2,2,2,64,128]{4,2,1,0,3:T(2,128)}), f32[2,2,2,64,128]{4,2,1,0,3:T(2,128)S(1)}, u32[]{:S(2)}, u32[]{:S(2)}) %all-to-all-start) | async-done | bytes 262176 | tf_op jit(solution)/shard_map/all_to_all | solution.py:123
  83.4 0.1 copy.70
  83.4 0.1 all_to_all.16
  83.6 0.9 multiply_reduce_fusion
  84.5 4.8 %fusion.7 = f32[5]{0:T(128)S(1)} fusion(f32[5,2,2,2,2,4096]{5,4,3,2,1,0:T(2,128)S(1)} %copy-done, f32[2,2,2,2,4096,1]{4,3,2,1,0,5:T(2,128)S(1)} %get-tuple-element.35), kind=kOutput, calls=%fused_computation.12 | convolution fusion | flops 3932160 | bytes 1572884 | tf_op jit(solution)/shard_map/dot_general | solution.py:127
  89.2 0.7 pad_maximum_fusion.2
  90.0 99.0 %all-reduce = (f32[5,5]{1,0:T(8,128)S(1)}, f32[6]{0:T(128)S(1)}) all-reduce(f32[5,5]{1,0:T(8,128)S(1)} %fusion.4, f32[6]{0:T(128)S(1)} %pad_maximum_fusion.2), channel_id=1, replica_groups=mesh['kgrp'=16,'energy'=32] {'kgrp','energy'}, use_global_device_ids=true, to_apply=%region_3.5 | all-reduce | flops 31 | bytes 248 | tf_op jit(solution)/shard_map/psum | solution.py:129
  189.0 0.0 copy-done.7
  189.0 0.2 fusion.27
  189.2 0.1 maximum_bitcast_fusion
  189.3 0.1 copy.73
  189.4 0.2 fusion.26
  189.6 0.2 fusion.25
  189.8 0.1 maximum_multiply_fusion
  189.9 0.2 fusion.29
  190.1 0.2 convolution_bitcast_fusion.1
  190.3 0.8 select_reduce_fusion.1
  191.1 0.1 copy.74
  191.8 0.4 cholesky.21
  192.3 0.6 compare_reduce_fusion
  193.0 0.6 select_select_fusion
  193.6 0.7 fusion.45
  194.3 0.7 fusion.47
  217.3 0.1 stack.35
  217.4 0.1 fusion.10
  217.6 0.2 convolution_bitcast_fusion.2
  217.7 0.7 fusion.46
  218.4 5.0 %bitcast_add_fusion = f32[2,2,2,2,4096]{4,3,2,1,0:T(2,128)} fusion(f32[5,2,2,2,2,4096]{5,4,3,2,1,0:T(2,128)S(1)} %copy-done, f32[5,2,2,2,2,4096]{5,4,3,2,1,0:T(2,128)S(1)} %copy-done.1, f32[2,2,2,2,4096]{4,3,2,1,0:T(2,128)S(1)} %copy-done.3, f32[]{:T(128)} %bitcast.88, f32[]{:T(128)} %bitcast.86, f32[]{:T(128)} %bitcast.84, f32[]{:T(128)} %bitcast.82, ...), kind=kLoop, calls=%fused_computation.17 | loop fusion | flops 1572864 | bytes 3407896 | tf_op jit(solution)/shard_map/add | solution.py:150
  (20 shorter events, 0.2 us)
Async XLA Ops:
  0.0 20.9 %copy-start.2 = (f32[2,2,2,64,128]{4,3,2,1,0:T(8,128)S(1)}, f32[2,2,2,64,128]{4,3,2,1,0:T(8,128)}, u32[]{:S(2)}) copy-start(f32[2,2,2,64,128]{4,3,2,1,0:T(8,128)} %param.16) | copy-start | bytes 786436
  1.2 19.6 %collective-permute-start = (f32[2,2,2,64,128]{4,2,3,1,0:T(2,128)S(1)}, f32[2,2,2,64,128]{4,2,3,1,0:T(2,128)S(1)}, u32[]{:S(2)}, u32[]{:S(2)}) collective-permute-start(f32[2,2,2,64,128]{4,2,3,1,0:T(2,128)S(1)} %copy.61), channel_id=1, source_target_pairs={{0,32},{32,64},{64,96},{96,128},{128,160},{160,192},{192,224},{224... | collective-permute-start | bytes 786440 | tf_op jit(solution)/shard_map/ppermute | solution.py:19
  5.2 15.9 %collective-permute-start.1 = (f32[2,2,2,64,128]{4,2,3,1,0:T(2,128)S(1)}, f32[2,2,2,64,128]{4,2,3,1,0:T(2,128)S(1)}, u32[]{:S(2)}, u32[]{:S(2)}) collective-permute-start(f32[2,2,2,64,128]{4,2,3,1,0:T(2,128)S(1)} %copy.61), channel_id=1, source_target_pairs={{32,0},{64,32},{96,64},{128,96},{160,128},{192,160},{224,192},{256... | collective-permute-start | bytes 786440 | tf_op jit(solution)/shard_map/ppermute | solution.py:22
  25.7 13.4 %copy-start.4 = (f32[2]{0:T(128)S(1)}, f32[2]{0:T(128)}, u32[]{:S(2)}) copy-start(f32[2]{0:T(128)} %param.25) | copy-start | bytes 28
  25.8 14.0 %copy-start.5 = (f32[4]{0:T(128)S(1)}, f32[4]{0:T(128)}, u32[]{:S(2)}) copy-start(f32[4]{0:T(128)} %param.24) | copy-start | bytes 52
  25.8 14.0 %copy-start.6 = (s32[64]{0:T(128)S(1)}, s32[64]{0:T(128)}, u32[]{:S(2)}) copy-start(s32[64]{0:T(128)} %param.22) | copy-start | bytes 772
  29.5 10.4 %collective-permute-start.2 = (f32[2,2,2,64,96]{4,3,2,1,0:T(8,128)S(1)}, f32[2,2,2,64,96]{4,3,2,1,0:T(8,128)S(1)}, u32[]{:S(2)}, u32[]{:S(2)}) collective-permute-start(f32[2,2,2,64,96]{4,3,2,1,0:T(8,128)S(1)} %get-tuple-element.36), channel_id=1, source_target_pairs={{0,1},{1,2},{2,3},{3,4},{4,5},{5,6},{6,7},{7,8},{8,9},{9,10},{10,1... | collective-permute-start | bytes 589832 | tf_op jit(solution)/shard_map/ppermute | solution.py:19
  34.0 7.7 %collective-permute-start.3 = (f32[2,2,2,64,96]{4,3,2,1,0:T(8,128)S(1)}, f32[2,2,2,64,96]{4,3,2,1,0:T(8,128)S(1)}, u32[]{:S(2)}, u32[]{:S(2)}) collective-permute-start(f32[2,2,2,64,96]{4,3,2,1,0:T(8,128)S(1)} %get-tuple-element.37), channel_id=1, source_target_pairs={{1,0},{2,1},{3,2},{4,3},{5,4},{6,5},{7,6},{8,7},{9,8},{10,9},{11,1... | collective-permute-start | bytes 589832 | tf_op jit(solution)/shard_map/ppermute | solution.py:22
  42.2 19.2 %copy-start = (f32[5,2,2,2,2,4096]{5,4,3,2,1,0:T(2,128)S(1)}, f32[5,2,2,2,2,4096]{5,4,3,2,1,0:T(2,128)}, u32[]{:S(2)}) copy-start(f32[5,2,2,2,2,4096]{5,4,3,2,1,0:T(2,128)} %param.19) | copy-start | bytes 3932164
  46.1 37.2 %all-to-all-start = ((f32[2,2,2,64,128]{4,2,1,0,3:T(2,128)}), f32[2,2,2,64,128]{4,2,1,0,3:T(2,128)S(1)}, u32[]{:S(2)}, u32[]{:S(2)}) async-start(f32[2,2,2,64,128]{4,2,1,0,3:T(2,128)} %copy.69), calls=%async_computation | async-start | bytes 524288 | tf_op jit(solution)/shard_map/all_to_all | solution.py:123
  61.4 22.2 %copy-start.3 = (f32[2,2,2,2,4096]{4,3,2,1,0:T(2,128)S(1)}, f32[2,2,2,2,4096]{4,3,2,1,0:T(2,128)}, u32[]{:S(2)}) copy-start(f32[2,2,2,2,4096]{4,3,2,1,0:T(2,128)} %param.17) | copy-start | bytes 786436
  84.5 104.5 %copy-start.7 = (s32[5]{0:T(128)S(1)}, s32[5]{0:T(128)}, u32[]{:S(2)}) copy-start(s32[5]{0:T(128)} %param.20) | copy-start | bytes 64
  84.5 132.9 %copy-start.8 = (f32[6]{0:T(128)S(1)}, f32[6]{0:T(128)}, u32[]{:S(2)}) copy-start(f32[6]{0:T(128)} %constant.127.clone.1) | copy-start | bytes 76
  84.5 133.9 %copy-start.1 = (f32[5,2,2,2,2,4096]{5,4,3,2,1,0:T(2,128)S(1)}, f32[5,2,2,2,2,4096]{5,4,3,2,1,0:T(2,128)}, u32[]{:S(2)}) copy-start(f32[5,2,2,2,2,4096]{5,4,3,2,1,0:T(2,128)} %param.18) | copy-start | bytes 3932164
where the time goes:
time: 224 us; the launch traced here: 223 us
  blocking collectives  99 us (44%)
  starting transfers between devices  34.5 us (15%)
  between operations  28.3 us (13%)
  waiting for transfers between devices  18.6 us (8%)
  other arithmetic  16.3 us (7%)
  local copies, waits for them, and re-layouts  14.7 us (7%)
  matrix products  12 us (5%)
    psum x1, blocking collectives, per_device(): lax.psum((jnp.dot(history, history.T, precision=lax.Precision.HIGHEST), n...  99 us
    all_to_all x1, waiting for transfers between devices, per_device(): lax.all_to_all(sigma_slice, 'energy', split_axis=3, concat_axis=4, tiled=...  16.8 us
    all_to_all x1, starting transfers between devices, per_device(): lax.all_to_all(sigma_slice, 'energy', split_axis=3, concat_axis=4, tiled=...  15.2 us
    ppermute x2, starting transfers between devices, padded_2(): lax.ppermute(lax.slice_in_dim(block, 0, width, axis=dim), axis, backward)  10.8 us
    ppermute x2, starting transfers between devices, padded_2(): lax.ppermute(lax.slice_in_dim(block, block.shape[dim] - width, None, axis...  8.46 us
    dot_general x1, matrix products, per_device(): jnp.dot(history, history.T, precision=lax.Precision.HIGHEST)  5.16 us
    add x1, other arithmetic, per_device(): mixed + slot_weights[column] * (past_inputs[column] + mixing_share * past...  4.95 us
    dot_general x1, matrix products, per_device(): jnp.dot(history, fresh, precision=lax.Precision.HIGHEST)  4.76 us
  transfers between devices with their start and end apart: 5, of which 2 were waited for; matrix products, arithmetic and copies ran while one was open for 5% of the time, Pallas kernels for 0%

commit v1 on v0

--- a/solution.py
+++ b/solution.py
@@ -127,8 +127,10 @@
         [jnp.sum(fresh * fresh)[None], jnp.dot(history, fresh, precision=lax.Precision.HIGHEST)]
     )
     old_products, new_products = lax.psum(
-        (jnp.dot(history, history.T, precision=lax.Precision.HIGHEST), new_local),
-        ("kgrp", "energy"),
+        lax.psum(
+            (jnp.dot(history, history.T, precision=lax.Precision.HIGHEST), new_local), "energy"
+        ),
+        "kgrp",
     )
     entries = float(fresh.shape[0] * lax.axis_size("kgrp") * lax.axis_size("energy"))
     reorder = (slot_order[:, None] == jnp.arange(HIST, dtype=jnp.int32)[None, :]).astype(

time: 224 us -> 208 us (0.929)
  the two profiles are of different devices: /device:TPU:1 before, /device:TPU:2 now
where the time goes in v1:
time: 208 us; the launch traced here: 207 us
  blocking collectives  86.6 us (42%)
  starting transfers between devices  30.5 us (15%)
  between operations  28.2 us (14%)
  waiting for transfers between devices  18.8 us (9%)
  other arithmetic  16.3 us (8%)
  local copies, waits for them, and re-layouts  14.6 us (7%)
  matrix products  12 us (6%)
    psum x1, blocking collectives, per_device(): lax.psum((jnp.dot(history, history.T, precision=lax.Precision.HIGHEST), n...  46.8 us
    psum x1, blocking collectives, per_device(): lax.psum(lax.psum((jnp.dot(history, history.T, precision=lax.Precision.HI...  39.8 us
    all_to_all x1, starting transfers between devices, per_device(): lax.all_to_all(sigma_slice, 'energy', split_axis=3, concat_axis=4, tiled=...  18.1 us
    all_to_all x1, waiting for transfers between devices, per_device(): lax.all_to_all(sigma_slice, 'energy', split_axis=3, concat_axis=4, tiled=...  17.4 us
    ppermute x2, starting transfers between devices, padded_2(): lax.ppermute(lax.slice_in_dim(block, 0, width, axis=dim), axis, backward)  7.63 us
    dot_general x1, matrix products, per_device(): jnp.dot(history, history.T, precision=lax.Precision.HIGHEST)  5.16 us
    add x1, other arithmetic, per_device(): mixed + slot_weights[column] * (past_inputs[column] + mixing_share * past...  5.03 us
    dot_general x1, matrix products, per_device(): jnp.dot(history, fresh, precision=lax.Precision.HIGHEST)  4.76 us
  transfers between devices with their start and end apart: 5, of which 2 were waited for; matrix products, arithmetic and copies ran while one was open for 5% of the time, Pallas kernels for 0%

profile of v1, /device:TPU:2, one launch (start us, length us, event | category | flops | bytes accessed | tf_op | source)
XLA Modules:
  0.0 206.9 jit_solution(520230912736645766)
XLA Ops:
  0.0 1.2 copy.61
  1.2 3.4 %collective-permute-start = (f32[2,2,2,64,128]{4,2,3,1,0:T(2,128)S(1)}, f32[2,2,2,64,128]{4,2,3,1,0:T(2,128)S(1)}, u32[]{:S(2)}, u32[]{:S(2)}) collective-permute-start(f32[2,2,2,64,128]{4,2,3,1,0:T(2,128)S(1)} %copy.61), channel_id=1, source_target_pairs={{0,32},{32,64},{64,96},{96,128},{128,160},{160,192},{192,224},{224... | collective-permute-start | bytes 786440 | tf_op jit(solution)/shard_map/ppermute | solution.py:19
  4.6 6.3 %collective-permute-start.1 = (f32[2,2,2,64,128]{4,2,3,1,0:T(2,128)S(1)}, f32[2,2,2,64,128]{4,2,3,1,0:T(2,128)S(1)}, u32[]{:S(2)}, u32[]{:S(2)}) collective-permute-start(f32[2,2,2,64,128]{4,2,3,1,0:T(2,128)S(1)} %copy.61), channel_id=1, source_target_pairs={{32,0},{64,32},{96,64},{128,96},{160,128},{192,160},{224,192},{256... | collective-permute-start | bytes 786440 | tf_op jit(solution)/shard_map/ppermute | solution.py:22
  11.0 0.7 add_select_fusion
  11.7 1.3 fusion.50
  13.0 1.3 fusion.49
  19.3 1.5 fusion.51
  20.8 0.0 collective-permute-done
  20.8 0.2 constant_dynamic-update-slice_fusion.1
  21.0 0.0 collective-permute-done.1
  21.1 0.9 gather_fusion.1
  22.0 0.9 gather_fusion.2
  22.9 0.9 gather_fusion.3
  23.9 0.9 gather_fusion.4
  24.8 0.9 gather_fusion
  25.7 0.0 copy-start.4
  25.7 0.0 copy-start.5
  25.7 0.0 copy-start.6
  25.7 3.5 %fusion.11 = f32[2,2,2,64,128]{4,3,2,1,0:T(8,128)S(1)} fusion(f32[64,2,2,2,128]{4,3,2,1,0:T(2,128)S(1)} %gather_fusion.4, f32[64,2,2,2,128]{4,3,2,1,0:T(2,128)S(1)} %gather_fusion.3, f32[64,2,2,2,128]{4,3,2,1,0:T(2,128)S(1)} %gather_fusion.2, f32[64,2,2,2,128]{4,3,2,1,0:T(2,128)S(1)} %gather_fusion.1, f32[64,2,2,2,128]{4,3,2,1,0:T(2,128)S(1)} %gather_fusion, ...), kind=kLoop, calls=%fused_computation.23 | loop fusion | flops 917504 | bytes 1573204 | tf_op jit(solution)/shard_map/add | solution.py:107
  29.2 0.1 fusion.44
  29.4 1.3 collective-permute-start.2
  30.7 1.3 collective-permute-start.3
  32.0 0.0 copy-done.4
  32.0 0.6 fusion.48
  32.6 0.0 copy-done.6
  32.6 0.1 select_reduce_fusion.2
  32.7 0.0 collective-permute-done.2
  32.7 1.4 collective-permute-done.3
  34.1 0.3 pad_maximum_fusion
  34.4 0.2 fusion.43
  34.6 0.0 copy-start
  34.6 3.0 %fusion.21 = (f32[1,2,2,64,128]{4,3,2,1,0:T(8,128)S(1)}, f32[1,2,2,64,128]{4,3,2,1,0:T(8,128)S(1)}) fusion(f32[2,2,64,320]{3,2,1,0:T(8,128)S(1)} %get-tuple-element.33, f32[1,2,2,64,320]{4,3,2,1,0:T(8,128)S(1)} %get-tuple-element.32, s32[]{:T(128)S(6)} %select_n.48, s32[]{:T(128)S(6)} %select_n.47, s32[]{:T(128)S(6)} %select_n.46, s32[]{:T(128)S(6)} %select_n.45, ...), kind=kLoop, calls=%fused_computation.45 | loop fusion | flops 720896 | bytes 1573160 | tf_op jit(solution)/shard_map/stack | solution.py:46
  37.7 0.9 copy.69
  38.6 18.1 %all-to-all-start = ((f32[2,2,2,64,128]{4,2,1,0,3:T(2,128)}), f32[2,2,2,64,128]{4,2,1,0,3:T(2,128)S(1)}, u32[]{:S(2)}, u32[]{:S(2)}) async-start(f32[2,2,2,64,128]{4,2,1,0,3:T(2,128)} %copy.69), calls=%async_computation | async-start | bytes 524288 | tf_op jit(solution)/shard_map/all_to_all | solution.py:123
  56.7 0.0 copy-start.3
  56.7 5.2 %fusion.4 = f32[5,5]{1,0:T(8,128)S(1)} fusion(f32[5,2,2,2,2,4096]{5,4,3,2,1,0:T(2,128)S(1)} %copy-done), kind=kOutput, calls=%fused_computation.9 | convolution fusion | flops 19660800 | bytes 1310820 | tf_op jit(solution)/shard_map/dot_general | solution.py:131
  61.9 17.4 %all-to-all-done = f32[2,2,2,64,128]{4,2,1,0,3:T(2,128)S(1)} async-done(((f32[2,2,2,64,128]{4,2,1,0,3:T(2,128)}), f32[2,2,2,64,128]{4,2,1,0,3:T(2,128)S(1)}, u32[]{:S(2)}, u32[]{:S(2)}) %all-to-all-start) | async-done | bytes 262176 | tf_op jit(solution)/shard_map/all_to_all | solution.py:123
  79.3 0.1 copy.70
  79.4 0.1 all_to_all.16
  79.5 0.9 multiply_reduce_fusion
  80.4 4.8 %fusion.7 = f32[5]{0:T(128)S(1)} fusion(f32[5,2,2,2,2,4096]{5,4,3,2,1,0:T(2,128)S(1)} %copy-done, f32[2,2,2,2,4096,1]{4,3,2,1,0,5:T(2,128)S(1)} %get-tuple-element.37), kind=kOutput, calls=%fused_computation.12 | convolution fusion | flops 3932160 | bytes 1572884 | tf_op jit(solution)/shard_map/dot_general | solution.py:127
  85.2 0.7 pad_maximum_fusion.2
  85.9 46.8 %all-reduce = (f32[5,5]{1,0:T(8,128)S(1)}, f32[6]{0:T(128)S(1)}) all-reduce(f32[5,5]{1,0:T(8,128)S(1)} %fusion.4, f32[6]{0:T(128)S(1)} %pad_maximum_fusion.2), channel_id=1, replica_groups=mesh['kgrp'=16,'energy'=32] {'energy'}, use_global_device_ids=true, to_apply=%region_4.6 | all-reduce | flops 31 | bytes 248 | tf_op jit(solution)/shard_map/psum | solution.py:130
  132.7 39.8 %all-reduce.1 = (f32[5,5]{1,0:T(8,128)S(1)}, f32[6]{0:T(128)S(1)}) all-reduce(f32[5,5]{1,0:T(8,128)S(1)} %get-tuple-element.18, f32[6]{0:T(128)S(1)} %get-tuple-element.19), channel_id=1, replica_groups=mesh['kgrp'=16,'energy'=32] {'kgrp'}, use_global_device_ids=true, to_apply=%region_5.7 | all-reduce | flops 31 | bytes 248 | tf_op jit(solution)/shard_map/psum | solution.py:129
  172.5 0.2 fusion.27
  172.7 0.1 maximum_bitcast_fusion
  172.8 0.1 copy.73
  172.9 0.2 fusion.26
  173.1 0.2 fusion.25
  173.3 0.1 maximum_multiply_fusion
  173.4 0.2 fusion.29
  173.6 0.2 convolution_bitcast_fusion.1
  173.8 0.8 select_reduce_fusion.1
  174.6 0.1 copy.74
  175.4 0.4 cholesky.21
  175.8 0.6 compare_reduce_fusion
  176.5 0.6 select_select_fusion
  177.1 0.7 fusion.45
  177.8 0.7 fusion.47
  200.8 0.1 stack.35
  200.9 0.1 fusion.10
  201.0 0.2 convolution_bitcast_fusion.2
  201.2 0.7 fusion.46
  201.9 5.0 %bitcast_add_fusion = f32[2,2,2,2,4096]{4,3,2,1,0:T(2,128)} fusion(f32[5,2,2,2,2,4096]{5,4,3,2,1,0:T(2,128)S(1)} %copy-done, f32[5,2,2,2,2,4096]{5,4,3,2,1,0:T(2,128)S(1)} %copy-done.1, f32[2,2,2,2,4096]{4,3,2,1,0:T(2,128)S(1)} %copy-done.3, f32[]{:T(128)} %bitcast.88, f32[]{:T(128)} %bitcast.86, f32[]{:T(128)} %bitcast.84, f32[]{:T(128)} %bitcast.82, ...), kind=kLoop, calls=%fused_computation.17 | loop fusion | flops 1572864 | bytes 3407896 | tf_op jit(solution)/shard_map/add | solution.py:152
  (21 shorter events, 0.2 us)
Async XLA Ops:
  0.0 20.8 %copy-start.2 = (f32[2,2,2,64,128]{4,3,2,1,0:T(8,128)S(1)}, f32[2,2,2,64,128]{4,3,2,1,0:T(8,128)}, u32[]{:S(2)}) copy-start(f32[2,2,2,64,128]{4,3,2,1,0:T(8,128)} %param.16) | copy-start | bytes 786436
  1.2 19.6 %collective-permute-start = (f32[2,2,2,64,128]{4,2,3,1,0:T(2,128)S(1)}, f32[2,2,2,64,128]{4,2,3,1,0:T(2,128)S(1)}, u32[]{:S(2)}, u32[]{:S(2)}) collective-permute-start(f32[2,2,2,64,128]{4,2,3,1,0:T(2,128)S(1)} %copy.61), channel_id=1, source_target_pairs={{0,32},{32,64},{64,96},{96,128},{128,160},{160,192},{192,224},{224... | collective-permute-start | bytes 786440 | tf_op jit(solution)/shard_map/ppermute | solution.py:19
  4.6 16.4 %collective-permute-start.1 = (f32[2,2,2,64,128]{4,2,3,1,0:T(2,128)S(1)}, f32[2,2,2,64,128]{4,2,3,1,0:T(2,128)S(1)}, u32[]{:S(2)}, u32[]{:S(2)}) collective-permute-start(f32[2,2,2,64,128]{4,2,3,1,0:T(2,128)S(1)} %copy.61), channel_id=1, source_target_pairs={{32,0},{64,32},{96,64},{128,96},{160,128},{192,160},{224,192},{256... | collective-permute-start | bytes 786440 | tf_op jit(solution)/shard_map/ppermute | solution.py:22
  25.7 6.3 %copy-start.4 = (f32[2]{0:T(128)S(1)}, f32[2]{0:T(128)}, u32[]{:S(2)}) copy-start(f32[2]{0:T(128)} %param.25) | copy-start | bytes 28
  25.7 6.9 %copy-start.5 = (f32[4]{0:T(128)S(1)}, f32[4]{0:T(128)}, u32[]{:S(2)}) copy-start(f32[4]{0:T(128)} %param.24) | copy-start | bytes 52
  25.7 6.9 %copy-start.6 = (s32[64]{0:T(128)S(1)}, s32[64]{0:T(128)}, u32[]{:S(2)}) copy-start(s32[64]{0:T(128)} %param.22) | copy-start | bytes 772
  29.4 3.3 %collective-permute-start.2 = (f32[2,2,2,64,96]{4,3,2,1,0:T(8,128)S(1)}, f32[2,2,2,64,96]{4,3,2,1,0:T(8,128)S(1)}, u32[]{:S(2)}, u32[]{:S(2)}) collective-permute-start(f32[2,2,2,64,96]{4,3,2,1,0:T(8,128)S(1)} %get-tuple-element.38), channel_id=1, source_target_pairs={{0,1},{1,2},{2,3},{3,4},{4,5},{5,6},{6,7},{7,8},{8,9},{9,10},{10,1... | collective-permute-start | bytes 589832 | tf_op jit(solution)/shard_map/ppermute | solution.py:19
  30.7 3.4 %collective-permute-start.3 = (f32[2,2,2,64,96]{4,3,2,1,0:T(8,128)S(1)}, f32[2,2,2,64,96]{4,3,2,1,0:T(8,128)S(1)}, u32[]{:S(2)}, u32[]{:S(2)}) collective-permute-start(f32[2,2,2,64,96]{4,3,2,1,0:T(8,128)S(1)} %get-tuple-element.39), channel_id=1, source_target_pairs={{1,0},{2,1},{3,2},{4,3},{5,4},{6,5},{7,6},{8,7},{9,8},{10,9},{11,1... | collective-permute-start | bytes 589832 | tf_op jit(solution)/shard_map/ppermute | solution.py:22
  34.6 22.1 %copy-start = (f32[5,2,2,2,2,4096]{5,4,3,2,1,0:T(2,128)S(1)}, f32[5,2,2,2,2,4096]{5,4,3,2,1,0:T(2,128)}, u32[]{:S(2)}) copy-start(f32[5,2,2,2,2,4096]{5,4,3,2,1,0:T(2,128)} %param.19) | copy-start | bytes 3932164
  38.6 40.7 %all-to-all-start = ((f32[2,2,2,64,128]{4,2,1,0,3:T(2,128)}), f32[2,2,2,64,128]{4,2,1,0,3:T(2,128)S(1)}, u32[]{:S(2)}, u32[]{:S(2)}) async-start(f32[2,2,2,64,128]{4,2,1,0,3:T(2,128)} %copy.69), calls=%async_computation | async-start | bytes 524288 | tf_op jit(solution)/shard_map/all_to_all | solution.py:123
  56.7 22.8 %copy-start.3 = (f32[2,2,2,2,4096]{4,3,2,1,0:T(2,128)S(1)}, f32[2,2,2,2,4096]{4,3,2,1,0:T(2,128)}, u32[]{:S(2)}) copy-start(f32[2,2,2,2,4096]{4,3,2,1,0:T(2,128)} %param.17) | copy-start | bytes 786436
  80.4 92.1 %copy-start.7 = (s32[5]{0:T(128)S(1)}, s32[5]{0:T(128)}, u32[]{:S(2)}) copy-start(s32[5]{0:T(128)} %param.20) | copy-start | bytes 64
  80.4 120.5 %copy-start.8 = (f32[6]{0:T(128)S(1)}, f32[6]{0:T(128)}, u32[]{:S(2)}) copy-start(f32[6]{0:T(128)} %constant.127.clone.1) | copy-start | bytes 76
  80.4 121.5 %copy-start.1 = (f32[5,2,2,2,2,4096]{5,4,3,2,1,0:T(2,128)S(1)}, f32[5,2,2,2,2,4096]{5,4,3,2,1,0:T(2,128)}, u32[]{:S(2)}) copy-start(f32[5,2,2,2,2,4096]{5,4,3,2,1,0:T(2,128)} %param.18) | copy-start | bytes 3932164
